TPU v7x, 32 devices: a whole 2x2x4 slice. The times are simulated.
32 devices in a mesh: view: 4 (over z), tile: 8 (over y, x, core).
Axes of the slice: x: 2, y: 2, z: 4, core: 2. Of those that a mesh axis runs over, the one named last changes fastest.
Arguments:
- centres: float32 [3, 32768], P(None, ('view', 'tile')), may hold values from -6 to 6
- shape_raw: float32 [6, 32768], P(None, ('view', 'tile')), may hold values from -1 to 0.2
- opacity_logit: float32 [32768], P(('view', 'tile')), may hold values from -6 to -1
- colours: float32 [3, 32768], P(None, ('view', 'tile')), may hold values from -6 to 6
- camera: float32 [8, 2, 4], replicated, may hold values from -15 to 15
- target: float32 [8, 128, 3, 256], P('view', 'tile'), may hold values from -3 to 3
- intersection_ids: int32 [8, 128, 256], P('view', 'tile'), may hold values from 0 to 32767, as said below
- depth_order: int32 [8, 128, 256], P('view', 'tile'), may hold values from 0 to 255, each once within a row
- live_count: int32 [8, 128], P('view', 'tile'), may hold values from 1 to 256, as said below
Outputs:
- rendered: float32 [8, 128, 3, 256], P('view', 'tile')
- grad_centres: float32 [3, 32768], P(None, ('view', 'tile'))
- grad_shape: float32 [6, 32768], P(None, ('view', 'tile'))
- grad_opacity: float32 [32768], P(('view', 'tile'))
- grad_colours: float32 [3, 32768], P(None, ('view', 'tile'))
- next_owner: int32 [8, 128], P('view', 'tile')
Inputs may be any that keep to these rules, and one draw needn't show every extreme that they name: `intersection_ids`: gaussian g is held by device g div 1024, devices counted along view+tile. Among the 2 x 16 x 256 slots held by one device at most 512 name Gaussians of any one device, and in every draw some device is named exactly 512 times by the slots of every device. `depth_order`: each tile's entries are a permutation of the slot numbers. Slot s of tile (v, t) is live when s < live_count[v, t]; every view has a tile with all 256 slots live.
All inputs are finite; a program needn't handle non-finite values.
Results may differ from a plain program's by a relative error of at most 0.0003.
Values sent between devices are 32-bit elements; how exact they have to be, the bound alone decides.
No kernel may reach another device: no remote copies, remote signals or barrier semaphores. Data moves between devices by JAX's collectives and lax.ppermute only.
A program may use at most 128 MiB of HBM per device.

v0:
```python
from functools import partial
import math
import jax
import jax.numpy as jnp
from jax import lax
from jax.sharding import PartitionSpec as P

SIDE = 16
exact_mode = lax.Precision.HIGHEST


def lower_factor(shape_raw):
    empty_cells = jnp.zeros_like(shape_raw[0])
    first_row = jnp.stack([jnp.exp(shape_raw[0]), empty_cells, empty_cells])
    second_row = jnp.stack([shape_raw[1], jnp.exp(shape_raw[2]), empty_cells])
    third_row = jnp.stack([shape_raw[3], shape_raw[4], jnp.exp(shape_raw[5])])
    return jnp.stack([first_row, second_row, third_row])


def project(centres, shape_raw, opacity_logit, colours, camera):
    view_count = camera.shape[0]
    gaussians = centres.shape[1]
    linear = camera[:, :, 0:3]
    screen = (
        jnp.einsum("vij,jg->vig", linear, centres, precision=exact_mode)
        + camera[:, :, 3][:, :, None]
    )
    factor = jnp.einsum("vik,kjg->vijg", linear, lower_factor(shape_raw), precision=exact_mode)
    var_x = jnp.sum(factor[:, 0] * factor[:, 0], axis=1) + 0.3
    cov_xy = jnp.sum(factor[:, 0] * factor[:, 1], axis=1)
    var_y = jnp.sum(factor[:, 1] * factor[:, 1], axis=1) + 0.3
    determinant = var_x * var_y - cov_xy * cov_xy
    opacity = 0.95 / (1.0 + jnp.exp(-opacity_logit))
    fields = [
        screen[:, 0],
        screen[:, 1],
        var_y / determinant,
        -cov_xy / determinant,
        var_x / determinant,
        jnp.broadcast_to(opacity, (view_count, gaussians)),
    ]
    for channel in range(3):
        fields.append(jnp.broadcast_to(colours[channel], (view_count, gaussians)))
    return jnp.stack(fields)


def pixel_offsets():
    pixel_index = jnp.arange(SIDE * SIDE, dtype=jnp.int32)
    across = (pixel_index % SIDE).astype(jnp.float32) - (SIDE - 1) / 2.0
    downward = (pixel_index // SIDE).astype(jnp.float32) - (SIDE - 1) / 2.0
    return (across, downward)


def render_tile(slot_rec, order, live_count):
    slot_count = order.shape[0]
    picker = (
        order[:, None] == lax.broadcasted_iota(jnp.int32, (slot_count, slot_count), 1)
    ).astype(jnp.float32)
    ordered = jnp.einsum("ks,js->kj", slot_rec, picker, precision=exact_mode)
    active_slots = (order < live_count).astype(jnp.float32)
    across, downward = pixel_offsets()
    delta_x = across[:, None] - ordered[0][None, :]
    delta_y = downward[:, None] - ordered[1][None, :]
    radius = (
        ordered[2] * delta_x * delta_x
        + 2.0 * ordered[3] * delta_x * delta_y
        + ordered[4] * delta_y * delta_y
    )
    coverage = active_slots * ordered[5] * jnp.exp(-0.5 * radius)
    keep_log = jnp.log1p(-coverage)
    earlier = (
        lax.broadcasted_iota(jnp.int32, (slot_count, slot_count), 0)
        < lax.broadcasted_iota(jnp.int32, (slot_count, slot_count), 1)
    ).astype(jnp.float32)
    through = jnp.exp(jnp.dot(keep_log, earlier, precision=exact_mode))
    weights = through * coverage
    return jnp.einsum("ck,pk->cp", ordered[6:9], weights, precision=exact_mode)


def render_block(slot_rec, order, live_count):
    return jax.vmap(render_tile)(slot_rec, order, live_count)


def render_all(slot_rec, order, live_count):
    lead_count, tile_count, slot_count = order.shape
    total_tiles = lead_count * tile_count
    block_size = math.gcd(total_tiles, 8)
    records = jnp.moveaxis(slot_rec, 0, 2).reshape(
        total_tiles // block_size, block_size, 9, slot_count
    )
    orders = order.reshape(total_tiles // block_size, block_size, slot_count)
    counts = live_count.reshape(total_tiles // block_size, block_size)
    blocked = jax.checkpoint(render_block)

    def one_block(packed):
        return blocked(packed[0], packed[1], packed[2])

    images = lax.map(one_block, (records, orders, counts))
    return images.reshape(lead_count, tile_count, 3, SIDE * SIDE)


def slot_ranks(owner_table):
    slots_here, devices = owner_table.shape
    block_rows = math.gcd(slots_here, 512)
    blocks = slots_here // block_rows
    grouped = owner_table.reshape(blocks, block_rows, devices)
    strict = (
        lax.broadcasted_iota(jnp.int32, (block_rows, block_rows), 1)
        < lax.broadcasted_iota(jnp.int32, (block_rows, block_rows), 0)
    ).astype(jnp.float32)
    inner = jnp.einsum("ij,njd->nid", strict, grouped, precision=exact_mode)
    block_totals = jnp.sum(grouped, axis=1)
    block_before = jnp.cumsum(block_totals, axis=0) - block_totals
    ranked = (inner + block_before[:, None, :]) * grouped
    return jnp.sum(ranked, axis=2).reshape(slots_here)


def fetch_rows(flat_rec, wanted):
    return jnp.take(flat_rec, wanted, axis=1)


def return_rows(values, wanted, columns):
    summed = jax.ops.segment_sum(jnp.transpose(values), wanted, num_segments=columns)
    return jnp.transpose(summed)


def shards(
    centres,
    shape_raw,
    opacity_logit,
    colours,
    camera,
    target,
    intersection_ids,
    depth_order,
    live_count,
):
    view_group = lax.axis_size("view")
    tile_group = lax.axis_size("tile")
    devices = view_group * tile_group
    own_count = centres.shape[1]
    views_here, tiles_here, slot_count = intersection_ids.shape
    slots_here = views_here * tiles_here * slot_count
    capacity = 2 * slots_here // devices
    totals = jnp.sum(live_count, axis=1)
    within = jnp.cumsum(live_count, axis=1) - live_count
    table = lax.all_gather(totals[None, :], "tile", axis=0, tiled=True)
    rank_rows = lax.broadcasted_iota(jnp.int32, table.shape, 0)
    before = jnp.sum(jnp.where(rank_rows < lax.axis_index("tile"), table, 0), axis=0)
    whole = jnp.sum(table, axis=0)
    next_owner = (before[:, None] + within) * tile_group // whole[:, None]
    project_here = partial(project, camera=camera)
    records, project_back = jax.vjp(project_here, centres, shape_raw, opacity_logit, colours)
    flat_rec = records.reshape(9, -1)
    rec_columns = flat_rec.shape[1]
    first_view = lax.axis_index("view") * views_here
    view_ids = first_view + lax.broadcasted_iota(jnp.int32, intersection_ids.shape, 0)
    owners = (intersection_ids // own_count).reshape(-1)
    request = (view_ids * own_count + intersection_ids % own_count).reshape(-1).astype(jnp.float32)
    peer_index = lax.broadcasted_iota(jnp.int32, (1, devices), 1)
    owner_table = (owners[:, None] == peer_index).astype(jnp.float32)
    ranks = slot_ranks(owner_table).astype(jnp.int32)
    rank_table = (ranks[:, None] == lax.broadcasted_iota(jnp.int32, (1, capacity), 1)).astype(
        jnp.float32
    )
    send_ids = (
        jnp.einsum("sd,sc->dc", owner_table, request[:, None] * rank_table, precision=exact_mode)
        .astype(jnp.int32)
        .reshape(-1)
    )
    got_ids = lax.all_to_all(send_ids, ("view", "tile"), split_axis=0, concat_axis=0, tiled=True)
    answer = fetch_rows(flat_rec, got_ids)
    fetched = lax.all_to_all(answer, ("view", "tile"), split_axis=1, concat_axis=1, tiled=True)
    by_rank = jnp.einsum(
        "kdc,sc->kds", fetched.reshape(9, devices, capacity), rank_table, precision=exact_mode
    )
    slot_rec = jnp.sum(by_rank * jnp.transpose(owner_table)[None], axis=1).reshape(
        9, views_here, tiles_here, slot_count
    )
    render_here = partial(render_all, order=depth_order, live_count=live_count)
    rendered, pullback = jax.vjp(render_here, slot_rec)
    slot_grad = pullback(rendered - target)[0].reshape(9, -1)
    weighted = slot_grad[:, :, None] * rank_table[None]
    back_buf = jnp.einsum("sd,ksc->kdc", owner_table, weighted, precision=exact_mode).reshape(
        9, devices * capacity
    )
    returned = lax.all_to_all(back_buf, ("view", "tile"), split_axis=1, concat_axis=1, tiled=True)
    record_grad = return_rows(returned, got_ids, rec_columns).reshape(records.shape)
    gradients = project_back(record_grad)
    return (rendered, gradients[0], gradients[1], gradients[2], gradients[3], next_owner)


def solution(mesh):
    in_specs = (
        P(None, ("view", "tile")),
        P(None, ("view", "tile")),
        P(("view", "tile")),
        P(None, ("view", "tile")),
        P(),
        P("view", "tile", None, None),
        P("view", "tile", None),
        P("view", "tile", None),
        P("view", "tile"),
    )
    out_specs = (
        P("view", "tile", None, None),
        P(None, ("view", "tile")),
        P(None, ("view", "tile")),
        P(("view", "tile")),
        P(None, ("view", "tile")),
        P("view", "tile"),
    )
    return jax.shard_map(shards, mesh=mesh, in_specs=in_specs, out_specs=out_specs, check_vma=False)
```

profile of v0, /device:TPU:0, one launch (start us, length us, event | category | flops | bytes accessed | tf_op | source)
XLA Modules:
  0.0 478.5 jit_solution(9977849283200208943)
XLA Ops:
  0.7 0.8 fusion.155
  2.4 7.6 %fusion.128 = s32[32,512,1]{1,0,2:T(8,128)S(1)} fusion(f32[8192]{0:T(1024)S(1)} %bitcast.348, s32[8192]{0:T(1024)S(1)} %bitcast.334, s32[8192]{0:T(1024)S(1)} %bitcast.324), kind=kOutput, calls=%fused_computation.182 | convolution fusion | flops 1619279872 | bytes 163840 | tf_op jit(solution)/shard_map/sd,sc->dc/dot_general | solution.py:167
  10.0 0.7 copy.67
  10.7 7.3 %all-to-all-start = ((s32[32,512,1]{1,2,0:T(1,128)}), s32[32,512,1]{1,2,0:T(1,128)S(1)}, u32[]{:S(2)}, u32[]{:S(2)}) async-start(s32[32,512,1]{1,2,0:T(1,128)} %copy.67), calls=%async_computation | async-start | bytes 131072 | tf_op jit(solution)/shard_map/all_to_all | solution.py:171
  18.2 6.1 %fusion.103 = f32[8192,512]{1,0:T(8,128)} fusion(s32[8192]{0:T(1024)S(1)} %bitcast.335), kind=kLoop, calls=%fused_computation.155 | loop fusion | flops 8388608 | bytes 16809984 | tf_op jit(solution)/shard_map/convert_element_type | solution.py:163
  26.5 2.7 copy.70
  29.3 56.6 %gather_fusion = f32[16384,9]{1,0:T(8,128)} fusion(f32[9,8192]{0,1:T(8,128)} %copy.70, s32[16384]{0:T(1024)S(1)} %broadcast_clamp_fusion), kind=kCustom, calls=%fused_computation | custom fusion | bytes 1245184 | tf_op jit(solution)/shard_map/jit(_take)/gather | solution.py:119
  85.9 5.2 %copy.71 = f32[9,32,512]{2,0,1:T(8,128)S(1)} copy(f32[9,32,512]{0,2,1:T(8,128)} %bitcast.307) | data formatting | bytes 1179648 | tf_op jit(solution)/shard_map/jit(_take)/gather | solution.py:119
  91.2 1.1 broadcast_select_fusion
  92.3 6.0 %all-to-all-start.1 = ((f32[9,32,512]{2,0,1:T(8,128)}), f32[9,32,512]{2,0,1:T(8,128)S(1)}, u32[]{:S(2)}, u32[]{:S(2)}) async-start(f32[9,32,512]{2,0,1:T(8,128)} %broadcast_select_fusion), calls=%async_computation.1 | async-start | bytes 2097152 | tf_op jit(solution)/shard_map/all_to_all | solution.py:173
  98.5 26.0 %all-to-all-done.1 = f32[9,32,512]{2,0,1:T(8,128)S(1)} async-done(((f32[9,32,512]{2,0,1:T(8,128)}), f32[9,32,512]{2,0,1:T(8,128)S(1)}, u32[]{:S(2)}, u32[]{:S(2)}) %all-to-all-start.1) | async-done | bytes 589856 | tf_op jit(solution)/shard_map/all_to_all | solution.py:173
  124.5 13.1 %fusion.114 = f32[9,8192]{1,0:T(8,128)S(1)} fusion(f32[32,8192]{1,0:T(8,128)S(1)} %fusion.135, s32[8192]{0:T(1024)S(1)} %bitcast.336, f32[9,32,512]{2,0,1:T(8,128)S(1)} %all-to-all-done.1), kind=kOutput, calls=%fused_computation.172 | convolution fusion | flops 14504353792 | bytes 1966080 | tf_op jit(solution)/shard_map/kdc,sc->kds/dot_general | solution.py:174
  138.4 30.5 %while.27 = (s32[]{:T(128)}, f32[4,8,3,256]{3,1,0,2:T(8,128)S(1)}, f32[4,8,9,256]{3,2,1,0:T(8,128)S(1)}, s32[4,8,256]{2,1,0:T(8,128)S(1)}, s32[4,8]{1,0:T(4,128)S(1)}, /*index=5*/s32[]{:T(128)}) while((s32[]{:T(128)}, f32[4,8,3,256]{3,1,0,2:T(8,128)S(1)}, f32[4,8,9,256]{3,2,1,0:T(8,128)S(1)}, s32[4,8,256]{2,1,0:T(8,128)S(1)}, ...), condition=%wide.region_8.9_spmd.clone, body=%wide.region_7.8_spmd.clone.sunk | while | flops 1700407296 | bytes 4864185 | solution.py:98
  138.4 1.3 fusion.240
  139.8 3.3 fusion.243
  143.1 2.9 fusion.244
  146.0 1.3 fusion.240
  147.4 3.3 fusion.243
  150.7 2.9 fusion.244
  153.6 1.3 fusion.240
  155.1 3.3 fusion.243
  158.3 2.9 fusion.244
  161.3 1.3 fusion.240
  162.7 3.3 fusion.243
  166.0 2.9 fusion.244
  169.0 62.0 %while.26 = (s32[]{:T(128)}, f32[4,8,9,256]{3,2,1,0:T(8,128)S(1)}, f32[4,8,9,256]{3,2,1,0:T(8,128)S(1)}, s32[4,8,256]{2,1,0:T(8,128)S(1)}, s32[4,8]{1,0:T(4,128)...) while((s32[]{:T(128)}, f32[4,8,9,256]{3,2,1,0:T(8,128)S(1)}, ...), condition=%wide.region_16.17_spmd, body=%wide.region_9.16_spmd.sunk | while | flops 3417032704 | bytes 11907285 | solution.py:98
  169.3 1.3 fusion.226
  170.7 2.7 fusion.230
  173.5 2.3 fusion.232
  175.8 1.9 fusion.229
  177.7 5.9 %fusion.231 = (f32[8,256]{1,0:T(8,128)S(1)}, f32[8,256]{1,0:T(8,128)S(1)}, f32[8,256]{1,0:T(8,128)S(1)}, f32[8,256]{1,0:T(8,128)S(1)}, f32[8,256]{1,0:T(8,128)S(1)}, /*index=5*/f32[8,256]{1,0:T(8,128)S(1)}) fusion(f32[8,256]{1,0:T(8,128)S(1)} %get-tuple-element.492, f32[256]{0:T(256)S(1)} %get-tuple-element.493, ...), kind=kOutput, calls=%fused_computation.30.clone.1 | convolution fusion | flops 1640550400 | bytes 4294656 | tf_op jit(solution)/shard_map/transpose(jvp())/while/body/eval_jaxpr/checkpoint/vmap()/dot_general | solution.py:75
  183.6 1.0 fusion.233
  184.7 1.3 fusion.226
  186.2 2.7 fusion.230
  188.9 2.3 fusion.232
  191.2 1.9 fusion.229
  193.1 5.9 %fusion.231 = (f32[8,256]{1,0:T(8,128)S(1)}, f32[8,256]{1,0:T(8,128)S(1)}, f32[8,256]{1,0:T(8,128)S(1)}, f32[8,256]{1,0:T(8,128)S(1)}, f32[8,256]{1,0:T(8,128)S(1)}, /*index=5*/f32[8,256]{1,0:T(8,128)S(1)}) fusion(f32[8,256]{1,0:T(8,128)S(1)} %get-tuple-element.492, f32[256]{0:T(256)S(1)} %get-tuple-element.493, ...), kind=kOutput, calls=%fused_computation.30.clone.1 | convolution fusion | flops 1640550400 | bytes 4294656 | tf_op jit(solution)/shard_map/transpose(jvp())/while/body/eval_jaxpr/checkpoint/vmap()/dot_general | solution.py:75
  199.0 1.0 fusion.233
  200.2 1.3 fusion.226
  201.6 2.7 fusion.230
  204.3 2.3 fusion.232
  206.6 1.9 fusion.229
  208.5 5.9 %fusion.231 = (f32[8,256]{1,0:T(8,128)S(1)}, f32[8,256]{1,0:T(8,128)S(1)}, f32[8,256]{1,0:T(8,128)S(1)}, f32[8,256]{1,0:T(8,128)S(1)}, f32[8,256]{1,0:T(8,128)S(1)}, /*index=5*/f32[8,256]{1,0:T(8,128)S(1)}) fusion(f32[8,256]{1,0:T(8,128)S(1)} %get-tuple-element.492, f32[256]{0:T(256)S(1)} %get-tuple-element.493, ...), kind=kOutput, calls=%fused_computation.30.clone.1 | convolution fusion | flops 1640550400 | bytes 4294656 | tf_op jit(solution)/shard_map/transpose(jvp())/while/body/eval_jaxpr/checkpoint/vmap()/dot_general | solution.py:75
  214.5 1.0 fusion.233
  215.6 1.3 fusion.226
  217.0 2.7 fusion.230
  219.8 2.3 fusion.232
  222.1 1.9 fusion.229
  224.0 5.9 %fusion.231 = (f32[8,256]{1,0:T(8,128)S(1)}, f32[8,256]{1,0:T(8,128)S(1)}, f32[8,256]{1,0:T(8,128)S(1)}, f32[8,256]{1,0:T(8,128)S(1)}, f32[8,256]{1,0:T(8,128)S(1)}, /*index=5*/f32[8,256]{1,0:T(8,128)S(1)}) fusion(f32[8,256]{1,0:T(8,128)S(1)} %get-tuple-element.492, f32[256]{0:T(256)S(1)} %get-tuple-element.493, ...), kind=kOutput, calls=%fused_computation.30.clone.1 | convolution fusion | flops 1640550400 | bytes 4294656 | tf_op jit(solution)/shard_map/transpose(jvp())/while/body/eval_jaxpr/checkpoint/vmap()/dot_general | solution.py:75
  229.9 1.0 fusion.233
  231.5 68.7 %fusion.121 = f32[9,32,512]{2,1,0:T(8,128)S(1)} fusion(f32[8192,512]{1,0:T(8,128)} %fusion.103, f32[9,8192]{1,0:T(8,128)S(1)} %bitcast.319, pred[8192,32,1]{0,1,2:T(32,128)(4,1)S(1)} %fusion.187), kind=kOutput, calls=%fused_computation.178 | convolution fusion | flops 14533263360 | bytes 17924096 | tf_op jit(solution)/shard_map/sd,ksc->kdc/dot_general | solution.py:184
  300.2 1.4 copy.80
  301.6 3.6 all-to-all-start.2
  306.8 10.4 %all-reduce.23 = s32[16]{0:T(128)S(1)} all-reduce(s32[16]{0:T(128)S(1)} %dynamic-update-slice), channel_id=2, replica_groups=mesh['view'=4,'tile'=8] {'tile'}, use_global_device_ids=true, to_apply=%add.23 | all-reduce | flops 16 | bytes 128
  317.6 0.8 and_select_fusion.4
  318.4 0.6 copy.83
  319.1 12.4 %all-to-all-done.2 = f32[9,32,512]{2,0,1:T(8,128)S(1)} async-done(((f32[9,32,512]{2,0,1:T(8,128)}), f32[9,32,512]{2,0,1:T(8,128)S(1)}, u32[]{:S(2)}, u32[]{:S(2)}) %all-to-all-start.2) | async-done | bytes 589856 | tf_op jit(solution)/shard_map/all_to_all | solution.py:187
  332.5 4.7 copy.82
  337.2 103.7 %scatter_custom_fusion = f32[8192,9]{1,0:T(8,128)} fusion(s32[16384]{0:T(1024)S(1)} %bitcast.317, f32[16384,9]{1,0:T(8,128)} %copy.82, f32[]{:T(128)} %constant.249.clone.1), kind=kCustom, calls=%fused_computation.173 | custom fusion | flops 147456 | bytes 295424 | tf_op jit(solution)/shard_map/scatter-add | solution.py:123
  440.9 32.8 %slice_reduce_fusion.2 = (f32[8192]{0:T(1024)S(1)}, f32[8192]{0:T(1024)S(1)}, f32[8192]{0:T(1024)S(1)}, f32[8192]{0:T(1024)S(1)}, f32[8192]{0:T(1024)S(1)}, /*in...) fusion(f32[9,8192]{0,1:T(8,128)} %bitcast.306), kind=kLoop, calls=%fused_computation.165 | loop fusion | bytes 589824 | tf_op jit(solution)/shard_map/transpose(jvp())/unstack | solution.py:44
  474.2 0.9 fusion.161
  475.9 0.8 convolution_bitcast_fusion.2
  476.8 0.6 pad_add_fusion.2
  477.4 0.6 pad_add_fusion.1
  (232 shorter events, 9.5 us)
Async XLA Ops:
  0.6 24.8 %copy-start = (f32[3,1024]{1,0:T(4,128)S(1)}, f32[3,1024]{1,0:T(4,128)}, u32[]{:S(2)}) copy-start(f32[3,1024]{1,0:T(4,128)} %param.13) | copy-start | bytes 36868
  2.4 15.7 %copy-start.13 = (f32[6,1024]{1,0:T(8,128)S(1)}, f32[6,1024]{1,0:T(8,128)}, u32[]{:S(2)}) copy-start(f32[6,1024]{1,0:T(8,128)} %param.14) | copy-start | bytes 73732
  10.7 18.5 %all-to-all-start = ((s32[32,512,1]{1,2,0:T(1,128)}), s32[32,512,1]{1,2,0:T(1,128)S(1)}, u32[]{:S(2)}, u32[]{:S(2)}) async-start(s32[32,512,1]{1,2,0:T(1,128)} %copy.67), calls=%async_computation | async-start | bytes 131072 | tf_op jit(solution)/shard_map/all_to_all | solution.py:171
  18.2 6.3 %copy-start.11 = (f32[8,2,4]{0,2,1:T(4,128)S(1)}, f32[8,2,4]{0,2,1:T(4,128)}, u32[]{:S(2)}) copy-start(f32[8,2,4]{0,2,1:T(4,128)} %param.17) | copy-start | bytes 772
  18.2 7.0 %copy-start.17 = (f32[3,1024]{1,0:T(4,128)S(1)}, f32[3,1024]{1,0:T(4,128)}, u32[]{:S(2)}) copy-start(f32[3,1024]{1,0:T(4,128)} %param.16) | copy-start | bytes 36868
  18.2 7.6 %copy-start.14 = (f32[1024]{0:T(1024)S(1)}, f32[1024]{0:T(1024)}, u32[]{:S(2)}) copy-start(f32[1024]{0:T(1024)} %param.15) | copy-start | bytes 12292
  24.9 1.0 copy-start.1
  25.0 1.0 copy-start.4
  25.0 1.0 copy-start.6
  25.0 1.0 copy-start.8
  26.4 2.7 copy-start.16
  92.3 32.2 %all-to-all-start.1 = ((f32[9,32,512]{2,0,1:T(8,128)}), f32[9,32,512]{2,0,1:T(8,128)S(1)}, u32[]{:S(2)}, u32[]{:S(2)}) async-start(f32[9,32,512]{2,0,1:T(8,128)} %broadcast_select_fusion), calls=%async_computation.1 | async-start | bytes 2097152 | tf_op jit(solution)/shard_map/all_to_all | solution.py:173
  137.6 0.8 copy-start.3
  138.4 30.5 %copy-start.10 = (f32[2,16,3,256]{3,1,2,0:T(8,128)S(1)}, f32[2,16,3,256]{3,1,2,0:T(8,128)}, u32[]{:S(2)}) copy-start(f32[2,16,3,256]{3,1,2,0:T(8,128)} %param.18) | copy-start | bytes 294916
  300.2 5.1 %copy-start.18 = (u32[32]{0:T(128)S(1)}, u32[32]{0:T(128)}, u32[]{:S(2)}) copy-start(u32[32]{0:T(128)} %constant.321) | copy-start | bytes 388
  301.6 29.8 %all-to-all-start.2 = ((f32[9,32,512]{2,0,1:T(8,128)}), f32[9,32,512]{2,0,1:T(8,128)S(1)}, u32[]{:S(2)}, u32[]{:S(2)}) async-start(f32[9,32,512]{2,0,1:T(8,128)} %copy.80), calls=%async_computation.2 | async-start | bytes 2097152 | tf_op jit(solution)/shard_map/all_to_all | solution.py:187
  440.9 32.9 %copy-start.5 = (f32[8,1024]{1,0:T(8,128)S(1)}, f32[8,1024]{1,0:T(8,128)}, u32[]{:S(2)}) copy-start(f32[8,1024]{1,0:T(8,128)} %copy-done.4) | copy-start | bytes 98308
  440.9 32.9 %copy-start.7 = (f32[8,1024]{1,0:T(8,128)S(1)}, f32[8,1024]{1,0:T(8,128)}, u32[]{:S(2)}) copy-start(f32[8,1024]{1,0:T(8,128)} %copy-done.6) | copy-start | bytes 98308
  440.9 32.9 %copy-start.9 = (f32[8,1024]{1,0:T(8,128)S(1)}, f32[8,1024]{1,0:T(8,128)}, u32[]{:S(2)}) copy-start(f32[8,1024]{1,0:T(8,128)} %copy-done.8) | copy-start | bytes 98308
  440.9 32.9 %copy-start.2 = (f32[8,2,3,1024]{3,0,1,2:T(8,128)S(1)}, f32[8,2,3,1024]{3,0,1,2:T(8,128)}, u32[]{:S(2)}) copy-start(f32[8,2,3,1024]{3,0,1,2:T(8,128)} %copy-done.1) | copy-start | bytes 589828
  440.9 33.0 %copy-start.12 = (f32[8,2,4]{0,2,1:T(4,128)S(1)}, f32[8,2,4]{0,2,1:T(4,128)}, u32[]{:S(2)}) copy-start(f32[8,2,4]{0,2,1:T(4,128)} %param.17) | copy-start | bytes 772
  473.7 1.6 copy-start.15
where the time goes:
time: 487 us; the launch traced here: 479 us
  matrix products  182 us (37%)
  other arithmetic  118 us (24%)
  local copies, waits for them, and re-layouts  110 us (23%)
  waiting for transfers between devices  38.4 us (8%)
  starting transfers between devices  17 us (3%)
  blocking collectives  10.4 us (2%)
    scatter-add x1, other arithmetic, return_rows(): jax.ops.segment_sum(jnp.transpose(values), wanted, num_segments=columns)  104 us
    dot_general x1, matrix products, shards(): jnp.einsum('sd,ksc->kdc', owner_table, weighted, precision=exact_mode)  68.7 us
    gather x2, local copies, waits for them, and re-layouts, fetch_rows(): return jnp.take(flat_rec, wanted, axis=1)  61.8 us
    dot_general x12, matrix products, render_tile(): through = jnp.exp(jnp.dot(keep_log, earlier, precision=exact_mode))  47.6 us
    another operation x10, local copies, waits for them, and re-layouts, project(): return jnp.stack(fields)  35.9 us
    dot_general x12, matrix products, render_tile(): return jnp.einsum('ck,pk->cp', ordered[6:9], weights, precision=exact_mode)  28.1 us
    all_to_all x1, waiting for transfers between devices, shards(): lax.all_to_all(answer, ('view', 'tile'), split_axis=1, concat_axis=1, til...  26 us
    dot_general x12, matrix products, render_tile(): ordered = jnp.einsum('ks,js->kj', slot_rec, picker, precision=exact_mode)  14.3 us
  transfers between devices with their start and end apart: 3, of which 2 were waited for; matrix products, arithmetic and copies ran while one was open for 3% of the time, Pallas kernels for 0%

commit v1 on v0

--- a/solution.py
+++ b/solution.py
@@ -170,7 +170,15 @@
     )
     got_ids = lax.all_to_all(send_ids, ("view", "tile"), split_axis=0, concat_axis=0, tiled=True)
     answer = fetch_rows(flat_rec, got_ids)
-    fetched = lax.all_to_all(answer, ("view", "tile"), split_axis=1, concat_axis=1, tiled=True)
+    fetched = jnp.concatenate(
+        lax.all_to_all(
+            jnp.stack(jnp.split(answer, lax.axis_size(("view", "tile")), axis=1)),
+            ("view", "tile"),
+            0,
+            0,
+        ),
+        axis=1,
+    )
     by_rank = jnp.einsum(
         "kdc,sc->kds", fetched.reshape(9, devices, capacity), rank_table, precision=exact_mode
     )

time: 487 us -> 520 us (1.068)
  local copies, waits for them, and re-layouts: 110 us -> 134 us
  other arithmetic: 118 us -> 128 us
    unnamed x66 -> x103, local copies, waits for them, and re-layouts: 3.78 us -> 26.3 us
    select_n x2, other arithmetic: 1.22 us -> 11.8 us  [fetch_rows(): return jnp.take(flat_rec, wanted, axis=1)]
    another operation x0 -> x2, local copies, waits for them, and re-layouts: none -> 6.82 us  [shards(): jnp.stack(jnp.split(answer, lax.axis_size(('view', 'tile')), axis=1))]
    gather x2 -> x1, local copies, waits for them, and re-layouts: 61.8 us -> 56.6 us  [fetch_rows(): return jnp.take(flat_rec, wanted, axis=1)]
where the time goes in v1:
time: 520 us; the launch traced here: 513 us
  matrix products  182 us (35%)
  local copies, waits for them, and re-layouts  134 us (26%)
  other arithmetic  128 us (25%)
  waiting for transfers between devices  38.4 us (7%)
  starting transfers between devices  17.1 us (3%)
  blocking collectives  10.4 us (2%)
    scatter-add x1, other arithmetic, return_rows(): jax.ops.segment_sum(jnp.transpose(values), wanted, num_segments=columns)  104 us
    dot_general x1, matrix products, shards(): jnp.einsum('sd,ksc->kdc', owner_table, weighted, precision=exact_mode)  68.9 us
    gather x1, local copies, waits for them, and re-layouts, fetch_rows(): return jnp.take(flat_rec, wanted, axis=1)  56.6 us
    dot_general x12, matrix products, render_tile(): through = jnp.exp(jnp.dot(keep_log, earlier, precision=exact_mode))  47.5 us
    another operation x10, local copies, waits for them, and re-layouts, project(): return jnp.stack(fields)  35.8 us
    dot_general x12, matrix products, render_tile(): return jnp.einsum('ck,pk->cp', ordered[6:9], weights, precision=exact_mode)  28.2 us
    unnamed x103, local copies, waits for them, and re-layouts  26.3 us
    all_to_all x1, waiting for transfers between devices, shards(): lax.all_to_all(jnp.stack(jnp.split(answer, lax.axis_size(('view', 'tile')...  26.1 us
  transfers between devices with their start and end apart: 3, of which 2 were waited for; matrix products, arithmetic and copies ran while one was open for 3% of the time, Pallas kernels for 0%

profile of v1, /device:TPU:0, one launch (start us, length us, event | category | flops | bytes accessed | tf_op | source)
XLA Modules:
  0.0 513.1 jit_solution(14760113837677416998)
XLA Ops:
  0.7 0.8 fusion.188
  2.4 7.6 %fusion.128 = s32[32,512,1]{1,0,2:T(8,128)S(1)} fusion(f32[8192]{0:T(1024)S(1)} %bitcast.474, s32[8192]{0:T(1024)S(1)} %bitcast.460, s32[8192]{0:T(1024)S(1)} %bitcast.450), kind=kOutput, calls=%fused_computation.183 | convolution fusion | flops 1619279872 | bytes 163840 | tf_op jit(solution)/shard_map/sd,sc->dc/dot_general | solution.py:167
  10.7 7.5 %all-to-all-start = ((s32[32,512,1]{1,2,0:T(1,128)}), s32[32,512,1]{1,2,0:T(1,128)S(1)}, u32[]{:S(2)}, u32[]{:S(2)}) async-start(s32[32,512,1]{1,2,0:T(1,128)} %copy.199), calls=%async_computation | async-start | bytes 131072 | tf_op jit(solution)/shard_map/all_to_all | solution.py:171
  18.4 6.1 %fusion.103 = f32[8192,512]{1,0:T(8,128)} fusion(s32[8192]{0:T(1024)S(1)} %bitcast.461), kind=kLoop, calls=%fused_computation.155 | loop fusion | flops 8388608 | bytes 16809984 | tf_op jit(solution)/shard_map/convert_element_type | solution.py:163
  26.6 2.7 copy.202
  29.5 56.6 %gather_fusion = f32[16384,9]{1,0:T(8,128)} fusion(f32[9,8192]{0,1:T(8,128)} %copy.202, s32[16384]{0:T(1024)S(1)} %broadcast_clamp_fusion), kind=kCustom, calls=%fused_computation | custom fusion | bytes 1245184 | tf_op jit(solution)/shard_map/jit(_take)/gather | solution.py:119
  86.1 11.8 %select_bitcast_fusion.1 = f32[9,16384]{0,1:T(8,128)S(1)} fusion(f32[16384,9]{1,0:T(8,128)} %gather_fusion, pred[16384]{0:T(1024)(128)(4,1)S(1)} %compare_and_fusion), kind=kLoop, calls=%fused_computation.159 | loop fusion | flops 147456 | bytes 1196032 | tf_op jit(solution)/shard_map/jit(_take)/select_n | solution.py:119
  100.8 0.7 fusion.168
  101.5 0.7 fusion.167
  106.6 0.7 fusion.160
  111.7 0.7 fusion.153
  121.1 6.1 %copy.203 = f32[32,9,512]{2,1,0:T(8,128)} copy(f32[32,9,512]{1,2,0:T(8,128)} %fusion.141) | data formatting | bytes 1179648 | tf_op jit(solution)/shard_map/stack | solution.py:175
  127.2 6.0 %all-to-all-start.1 = ((f32[32,9,512]{2,1,0:T(8,128)}), f32[32,9,512]{2,1,0:T(8,128)S(1)}, u32[]{:S(2)}, u32[]{:S(2)}) async-start(f32[32,9,512]{2,1,0:T(8,128)} %copy.203), calls=%async_computation.1 | async-start | bytes 2097152 | tf_op jit(solution)/shard_map/all_to_all | solution.py:174
  133.3 26.1 %all-to-all-done.1 = f32[32,9,512]{2,1,0:T(8,128)S(1)} async-done(((f32[32,9,512]{2,1,0:T(8,128)}), f32[32,9,512]{2,1,0:T(8,128)S(1)}, u32[]{:S(2)}, u32[]{:S(2)}) %all-to-all-start.1) | async-done | bytes 589856 | tf_op jit(solution)/shard_map/all_to_all | solution.py:174
  159.3 13.1 %fusion.114 = f32[9,8192]{1,0:T(8,128)S(1)} fusion(f32[32,8192]{1,0:T(8,128)S(1)} %fusion.135, s32[8192]{0:T(1024)S(1)} %bitcast.462, f32[32,9,512]{2,1,0:T(8,128)S(1)} %all-to-all-done.1), kind=kOutput, calls=%fused_computation.173 | convolution fusion | flops 14504353792 | bytes 1966080 | tf_op jit(solution)/shard_map/kdc,sc->kds/dot_general | solution.py:182
  173.2 30.5 %while.27 = (s32[]{:T(128)}, f32[4,8,3,256]{3,1,0,2:T(8,128)S(1)}, f32[4,8,9,256]{3,2,1,0:T(8,128)S(1)}, s32[4,8,256]{2,1,0:T(8,128)S(1)}, s32[4,8]{1,0:T(4,128)S(1)}, /*index=5*/s32[]{:T(128)}) while((s32[]{:T(128)}, f32[4,8,3,256]{3,1,0,2:T(8,128)S(1)}, f32[4,8,9,256]{3,2,1,0:T(8,128)S(1)}, s32[4,8,256]{2,1,0:T(8,128)S(1)}, ...), condition=%wide.region_8.9_spmd.clone, body=%wide.region_7.8_spmd.clone.sunk | while | flops 1700407296 | bytes 4864185 | solution.py:98
  173.2 1.3 fusion.273
  174.6 3.3 fusion.276
  177.9 2.9 fusion.277
  180.8 1.3 fusion.273
  182.2 3.3 fusion.276
  185.5 2.9 fusion.277
  188.4 1.3 fusion.273
  189.9 3.3 fusion.276
  193.2 2.9 fusion.277
  196.1 1.3 fusion.273
  197.5 3.3 fusion.276
  200.8 2.9 fusion.277
  203.8 61.9 %while.26 = (s32[]{:T(128)}, f32[4,8,9,256]{3,2,1,0:T(8,128)S(1)}, f32[4,8,9,256]{3,2,1,0:T(8,128)S(1)}, s32[4,8,256]{2,1,0:T(8,128)S(1)}, s32[4,8]{1,0:T(4,128)...) while((s32[]{:T(128)}, f32[4,8,9,256]{3,2,1,0:T(8,128)S(1)}, ...), condition=%wide.region_16.17_spmd, body=%wide.region_9.16_spmd.sunk | while | flops 3417032704 | bytes 11907285 | solution.py:98
  204.1 1.3 fusion.259
  205.5 2.7 fusion.263
  208.3 2.3 fusion.265
  210.6 1.9 fusion.262
  212.5 5.9 %fusion.264 = (f32[8,256]{1,0:T(8,128)S(1)}, f32[8,256]{1,0:T(8,128)S(1)}, f32[8,256]{1,0:T(8,128)S(1)}, f32[8,256]{1,0:T(8,128)S(1)}, f32[8,256]{1,0:T(8,128)S(1)}, /*index=5*/f32[8,256]{1,0:T(8,128)S(1)}) fusion(f32[8,256]{1,0:T(8,128)S(1)} %get-tuple-element.526, f32[256]{0:T(256)S(1)} %get-tuple-element.527, ...), kind=kOutput, calls=%fused_computation.30.clone.1 | convolution fusion | flops 1640550400 | bytes 4294656 | tf_op jit(solution)/shard_map/transpose(jvp())/while/body/eval_jaxpr/checkpoint/vmap()/dot_general | solution.py:75
  218.4 1.0 fusion.266
  219.5 1.3 fusion.259
  221.0 2.7 fusion.263
  223.7 2.3 fusion.265
  226.0 1.9 fusion.262
  227.9 5.9 %fusion.264 = (f32[8,256]{1,0:T(8,128)S(1)}, f32[8,256]{1,0:T(8,128)S(1)}, f32[8,256]{1,0:T(8,128)S(1)}, f32[8,256]{1,0:T(8,128)S(1)}, f32[8,256]{1,0:T(8,128)S(1)}, /*index=5*/f32[8,256]{1,0:T(8,128)S(1)}) fusion(f32[8,256]{1,0:T(8,128)S(1)} %get-tuple-element.526, f32[256]{0:T(256)S(1)} %get-tuple-element.527, ...), kind=kOutput, calls=%fused_computation.30.clone.1 | convolution fusion | flops 1640550400 | bytes 4294656 | tf_op jit(solution)/shard_map/transpose(jvp())/while/body/eval_jaxpr/checkpoint/vmap()/dot_general | solution.py:75
  233.8 1.0 fusion.266
  235.0 1.3 fusion.259
  236.4 2.7 fusion.263
  239.1 2.3 fusion.265
  241.5 1.9 fusion.262
  243.3 5.9 %fusion.264 = (f32[8,256]{1,0:T(8,128)S(1)}, f32[8,256]{1,0:T(8,128)S(1)}, f32[8,256]{1,0:T(8,128)S(1)}, f32[8,256]{1,0:T(8,128)S(1)}, f32[8,256]{1,0:T(8,128)S(1)}, /*index=5*/f32[8,256]{1,0:T(8,128)S(1)}) fusion(f32[8,256]{1,0:T(8,128)S(1)} %get-tuple-element.526, f32[256]{0:T(256)S(1)} %get-tuple-element.527, ...), kind=kOutput, calls=%fused_computation.30.clone.1 | convolution fusion | flops 1640550400 | bytes 4294656 | tf_op jit(solution)/shard_map/transpose(jvp())/while/body/eval_jaxpr/checkpoint/vmap()/dot_general | solution.py:75
  249.3 1.0 fusion.266
  250.4 1.3 fusion.259
  251.8 2.7 fusion.263
  254.6 2.3 fusion.265
  256.9 1.9 fusion.262
  258.8 5.9 %fusion.264 = (f32[8,256]{1,0:T(8,128)S(1)}, f32[8,256]{1,0:T(8,128)S(1)}, f32[8,256]{1,0:T(8,128)S(1)}, f32[8,256]{1,0:T(8,128)S(1)}, f32[8,256]{1,0:T(8,128)S(1)}, /*index=5*/f32[8,256]{1,0:T(8,128)S(1)}) fusion(f32[8,256]{1,0:T(8,128)S(1)} %get-tuple-element.526, f32[256]{0:T(256)S(1)} %get-tuple-element.527, ...), kind=kOutput, calls=%fused_computation.30.clone.1 | convolution fusion | flops 1640550400 | bytes 4294656 | tf_op jit(solution)/shard_map/transpose(jvp())/while/body/eval_jaxpr/checkpoint/vmap()/dot_general | solution.py:75
  264.7 1.0 fusion.266
  266.3 68.9 %fusion.121 = f32[9,32,512]{2,1,0:T(8,128)S(1)} fusion(f32[8192,512]{1,0:T(8,128)} %fusion.103, f32[9,8192]{1,0:T(8,128)S(1)} %bitcast.445, pred[8192,32,1]{0,1,2:T(32,128)(4,1)S(1)} %fusion.220), kind=kOutput, calls=%fused_computation.179 | convolution fusion | flops 14533263360 | bytes 17924096 | tf_op jit(solution)/shard_map/sd,ksc->kdc/dot_general | solution.py:192
  335.2 1.4 copy.212
  336.5 3.6 all-to-all-start.2
  341.8 10.4 %all-reduce.23 = s32[16]{0:T(128)S(1)} all-reduce(s32[16]{0:T(128)S(1)} %dynamic-update-slice), channel_id=2, replica_groups=mesh['view'=4,'tile'=8] {'tile'}, use_global_device_ids=true, to_apply=%add.23 | all-reduce | flops 16 | bytes 128
  352.6 0.8 and_select_fusion.4
  354.0 12.4 %all-to-all-done.2 = f32[9,32,512]{2,0,1:T(8,128)S(1)} async-done(((f32[9,32,512]{2,0,1:T(8,128)}), f32[9,32,512]{2,0,1:T(8,128)S(1)}, u32[]{:S(2)}, u32[]{:S(2)}) %all-to-all-start.2) | async-done | bytes 589856 | tf_op jit(solution)/shard_map/all_to_all | solution.py:195
  367.5 4.7 copy.214
  372.1 103.7 %scatter_custom_fusion = f32[8192,9]{1,0:T(8,128)} fusion(s32[16384]{0:T(1024)} %bitcast.443, f32[16384,9]{1,0:T(8,128)} %copy.214, f32[]{:T(128)} %constant.249.clone.1), kind=kCustom, calls=%fused_computation.174 | custom fusion | flops 147456 | bytes 295424 | tf_op jit(solution)/shard_map/scatter-add | solution.py:123
  475.9 32.6 %slice_reduce_fusion.2 = (f32[8192]{0:T(1024)S(1)}, f32[8192]{0:T(1024)S(1)}, f32[8192]{0:T(1024)S(1)}, f32[8192]{0:T(1024)S(1)}, f32[8192]{0:T(1024)S(1)}, /*in...) fusion(f32[9,8192]{0,1:T(8,128)} %bitcast.432), kind=kLoop, calls=%fused_computation.166 | loop fusion | bytes 589824 | tf_op jit(solution)/shard_map/transpose(jvp())/unstack | solution.py:44
  509.0 0.9 fusion.194
  510.8 0.8 convolution_bitcast_fusion.2
  (270 shorter events, 32.4 us)
Async XLA Ops:
  0.6 25.0 %copy-start = (f32[3,1024]{1,0:T(4,128)S(1)}, f32[3,1024]{1,0:T(4,128)}, u32[]{:S(2)}) copy-start(f32[3,1024]{1,0:T(4,128)} %param.13) | copy-start | bytes 36868
  2.4 15.9 %copy-start.15 = (f32[6,1024]{1,0:T(8,128)S(1)}, f32[6,1024]{1,0:T(8,128)}, u32[]{:S(2)}) copy-start(f32[6,1024]{1,0:T(8,128)} %param.14) | copy-start | bytes 73732
  10.7 18.6 %all-to-all-start = ((s32[32,512,1]{1,2,0:T(1,128)}), s32[32,512,1]{1,2,0:T(1,128)S(1)}, u32[]{:S(2)}, u32[]{:S(2)}) async-start(s32[32,512,1]{1,2,0:T(1,128)} %copy.199), calls=%async_computation | async-start | bytes 131072 | tf_op jit(solution)/shard_map/all_to_all | solution.py:171
  18.4 6.3 %copy-start.13 = (f32[8,2,4]{0,2,1:T(4,128)S(1)}, f32[8,2,4]{0,2,1:T(4,128)}, u32[]{:S(2)}) copy-start(f32[8,2,4]{0,2,1:T(4,128)} %param.17) | copy-start | bytes 772
  18.4 7.0 %copy-start.20 = (f32[3,1024]{1,0:T(4,128)S(1)}, f32[3,1024]{1,0:T(4,128)}, u32[]{:S(2)}) copy-start(f32[3,1024]{1,0:T(4,128)} %param.16) | copy-start | bytes 36868
  18.4 7.6 %copy-start.16 = (f32[1024]{0:T(1024)S(1)}, f32[1024]{0:T(1024)}, u32[]{:S(2)}) copy-start(f32[1024]{0:T(1024)} %param.15) | copy-start | bytes 12292
  25.1 1.0 copy-start.2
  25.2 4.1 copy-start.6
  25.2 4.1 copy-start.8
  25.2 4.1 copy-start.10
  26.6 2.7 copy-start.18
  29.4 56.7 %copy-start.4 = (s32[32,512,1]{1,2,0:T(1,128)}, s32[32,512,1]{1,2,0:T(1,128)S(1)}, u32[]{:S(2)}) copy-start(s32[32,512,1]{1,2,0:T(1,128)S(1)} %all-to-all-done) | copy-start | bytes 196612
  127.2 32.2 %all-to-all-start.1 = ((f32[32,9,512]{2,1,0:T(8,128)}), f32[32,9,512]{2,1,0:T(8,128)S(1)}, u32[]{:S(2)}, u32[]{:S(2)}) async-start(f32[32,9,512]{2,1,0:T(8,128)} %copy.203), calls=%async_computation.1 | async-start | bytes 2097152 | tf_op jit(solution)/shard_map/all_to_all | solution.py:174
  172.4 0.8 copy-start.5
  173.2 30.5 %copy-start.12 = (f32[2,16,3,256]{3,1,2,0:T(8,128)S(1)}, f32[2,16,3,256]{3,1,2,0:T(8,128)}, u32[]{:S(2)}) copy-start(f32[2,16,3,256]{3,1,2,0:T(8,128)} %param.18) | copy-start | bytes 294916
  335.2 5.0 copy-start.19
  335.2 5.1 %copy-start.21 = (u32[32]{0:T(128)S(1)}, u32[32]{0:T(128)}, u32[]{:S(2)}) copy-start(u32[32]{0:T(128)} %constant.321) | copy-start | bytes 388
  336.5 29.8 %all-to-all-start.2 = ((f32[9,32,512]{2,0,1:T(8,128)}), f32[9,32,512]{2,0,1:T(8,128)S(1)}, u32[]{:S(2)}, u32[]{:S(2)}) async-start(f32[9,32,512]{2,0,1:T(8,128)} %copy.212), calls=%async_computation.2 | async-start | bytes 2097152 | tf_op jit(solution)/shard_map/all_to_all | solution.py:195
  475.8 32.7 %copy-start.7 = (f32[8,1024]{1,0:T(8,128)S(1)}, f32[8,1024]{1,0:T(8,128)}, u32[]{:S(2)}) copy-start(f32[8,1024]{1,0:T(8,128)} %copy-done.6) | copy-start | bytes 98308
  475.8 32.8 %copy-start.9 = (f32[8,1024]{1,0:T(8,128)S(1)}, f32[8,1024]{1,0:T(8,128)}, u32[]{:S(2)}) copy-start(f32[8,1024]{1,0:T(8,128)} %copy-done.8) | copy-start | bytes 98308
  475.8 32.8 %copy-start.11 = (f32[8,1024]{1,0:T(8,128)S(1)}, f32[8,1024]{1,0:T(8,128)}, u32[]{:S(2)}) copy-start(f32[8,1024]{1,0:T(8,128)} %copy-done.10) | copy-start | bytes 98308
  475.8 32.8 %copy-start.3 = (f32[8,2,3,1024]{3,0,1,2:T(8,128)S(1)}, f32[8,2,3,1024]{3,0,1,2:T(8,128)}, u32[]{:S(2)}) copy-start(f32[8,2,3,1024]{3,0,1,2:T(8,128)} %copy-done.2) | copy-start | bytes 589828
  475.8 32.9 %copy-start.14 = (f32[8,2,4]{0,2,1:T(4,128)S(1)}, f32[8,2,4]{0,2,1:T(4,128)}, u32[]{:S(2)}) copy-start(f32[8,2,4]{0,2,1:T(4,128)} %param.17) | copy-start | bytes 772
  475.9 37.0 %copy-start.1 = (f32[3,1024]{1,0:T(4,128)S(1)}, f32[3,1024]{1,0:T(4,128)}, u32[]{:S(2)}) copy-start(f32[3,1024]{1,0:T(4,128)} %param.13) | copy-start | bytes 36868
  508.5 1.6 copy-start.17
